TPU v7x, 32 devices: a whole 2x2x4 slice. The times are simulated.
32 devices in a mesh: egrp: 2 (over x), space: 16 (over z, y, core).
Axes of the slice: x: 2, y: 2, z: 4, core: 2. Of those that a mesh axis runs over, the one named last changes fastest.
Arguments:
- dist: float32 [2, 1024, 64, 128], P(None, 'egrp', 'space'), may hold values from -12 to 12
- hist_x: bfloat16 [4, 2, 1024, 64, 128], P(None, None, 'egrp', 'space'), may hold values from -6 to 6
- hist_g: bfloat16 [4, 2, 1024, 64, 128], P(None, None, 'egrp', 'space'), may hold values from -12 to 12
- mobility: float32 [64, 128], P('space'), may hold values from 0.2 to 2
- region: int32 [64, 128], P('space'), may hold values from 0 to 3
- phonon_bins: int32 [4], replicated, may hold values from 48 to 64, as said below
- coupling: float32 [4], replicated, may hold values from 0.2 to 1.5
- hist_used: int32 [2, 4], replicated, may hold values 0 or 1
Outputs:
- drifted: float32 [2, 1024, 64, 128], P(None, 'egrp', 'space')
Inputs may be any that keep to these rules, and one draw needn't show every extreme that they name: `phonon_bins`: each value lies in 48 to 64; both ends occur.
All inputs are finite; a program needn't handle non-finite values.
Results may differ from a plain program's by a relative error of at most 0.0003.
Values sent between devices are 32-bit elements; how exact they have to be, the bound alone decides.
A program may use at most 128 MiB of HBM per device.

v0:
```python
import jax
import jax.numpy as jnp
from jax import lax
from jax.sharding import PartitionSpec as P

NE = 1024
HISTORY = 4
NREGION = 4
KMAX = 64
COLS = 64


def extended(block, sides, width):
    for axis, dim in sides:
        count = lax.axis_size(axis)
        forward = [(i, i + 1) for i in range(count - 1)]
        backward = [(target, source) for source, target in forward]
        low = lax.ppermute(
            lax.slice_in_dim(block, block.shape[dim] - width, None, axis=dim), axis, forward
        )
        high = lax.ppermute(lax.slice_in_dim(block, 0, width, axis=dim), axis, backward)
        block = jnp.concatenate([low, block, high], axis=dim)
    return block


def add_face(total, field, moved, mobility, moved_mob, valid):
    return total + jnp.where(valid, 0.5 * (mobility + moved_mob) * (moved - field), 0.0)


def local(dist, hist_x, hist_g, mobility, region, phonon_bins, coupling, hist_used):
    width = dist.shape[1]
    rows = dist.shape[2]
    cells = dist.shape[3]
    flat_g = hist_g.reshape(HISTORY, 2, -1)
    energy_ids = lax.axis_index("egrp") * width + jnp.arange(width, dtype=jnp.int32)
    dos = jnp.sqrt((energy_ids.astype(jnp.float32) + 0.5) / NE)
    even = dist[0]
    odd = dist[1]
    outrate = jnp.zeros(even.shape, jnp.float32)
    lam = jnp.zeros(region.shape, jnp.float32)
    for index in range(NREGION):
        offset = phonon_bins[index]
        lower = energy_ids - offset
        upper = energy_ids + offset
        dos_low = jnp.where(
            lower >= 0, jnp.sqrt((jnp.maximum(lower, 0).astype(jnp.float32) + 0.5) / NE), 0.0
        )
        dos_high = jnp.where(upper < NE, jnp.sqrt((upper.astype(jnp.float32) + 0.5) / NE), 0.0)
        rate = coupling[index] * (1.5 * dos_low + 0.5 * dos_high)
        outrate = jnp.where((region == index)[None], rate[:, None, None], outrate)
        lam = jnp.where(region == index, coupling[index], lam)
    column = lax.all_to_all(
        even.reshape(width, rows * cells), "egrp", split_axis=1, concat_axis=0, tiled=True
    )
    span = column.shape[1]
    column_region = lax.dynamic_slice_in_dim(
        region.reshape(-1), lax.axis_index("egrp") * span, span
    )
    padded = jnp.pad(column, ((KMAX, KMAX), (0, 0)))
    total = column.shape[0]
    partial_sum = jnp.zeros(column.shape, jnp.float32)
    for index in range(NREGION):
        offset = phonon_bins[index]
        above = lax.dynamic_slice_in_dim(padded, KMAX + offset, total, 0)
        below = lax.dynamic_slice_in_dim(padded, KMAX - offset, total, 0)
        partial_sum = jnp.where(
            (column_region == index)[None], 1.5 * above + 0.5 * below, partial_sum
        )
    shifted = lax.all_to_all(partial_sum, "egrp", split_axis=0, concat_axis=1, tiled=True).reshape(
        width, rows, cells
    )
    gain_in = lam[None] * dos[:, None, None] * shifted
    new_even = (even + gain_in) / (1.0 + outrate)
    new_odd = odd / (1.0 + outrate + lam[None])
    res = jnp.stack([new_even - even, new_odd - odd])
    res_flat = res.reshape(2, -1)
    cross = jnp.transpose(jnp.sum(flat_g.astype(jnp.float32) * res_flat[None], axis=2))
    self_term = jnp.sum(res_flat * res_flat, axis=1)
    among = lax.dot_general(
        flat_g, flat_g, (((2,), (2,)), ((1,), (1,))), preferred_element_type=jnp.float32
    )
    among, cross, self_term = lax.psum((among, cross, self_term), ("egrp", "space"))
    fields = []
    for field in range(2):
        top = jnp.concatenate([self_term[field][None], cross[field]])[None, :]
        lower_rows = jnp.concatenate([cross[field][:, None], among[field]], axis=1)
        gram = jnp.concatenate([top, lower_rows], axis=0)
        valid = jnp.concatenate([jnp.ones((1,), jnp.float32), hist_used[field].astype(jnp.float32)])
        masked = valid[:, None] * valid[None, :] * gram + jnp.diag(1.0 - valid) * gram[0, 0]
        factor = jnp.linalg.cholesky(masked)
        weights = jax.scipy.linalg.cho_solve((factor, True), valid)
        coeffs = weights / jnp.sum(weights)
        part_mix = coeffs[0] * (dist[field] + 0.5 * res[field])
        for index in range(HISTORY):
            part_mix = part_mix + coeffs[index + 1] * (
                hist_x[index, field].astype(jnp.float32)
                + 0.5 * hist_g[index, field].astype(jnp.float32)
            )
        fields.append(part_mix)
    mixed = jnp.stack(fields)
    mob_block = mobility[None, None]
    wide_field, wide_mob = (
        extended(mixed, (("space", 2),), 1),
        extended(mob_block, (("space", 2),), 1),
    )
    row_ids = lax.axis_index("space") * rows + jnp.arange(rows, dtype=jnp.int32)
    all_rows = lax.axis_size("space") * rows
    cell_ids = jnp.arange(cells, dtype=jnp.int32)
    column_ids = cell_ids % COLS
    lap = jnp.zeros(mixed.shape, jnp.float32)
    lap = add_face(
        lap,
        mixed,
        wide_field[:, :, 0:rows],
        mob_block,
        wide_mob[:, :, 0:rows],
        (row_ids > 0)[:, None],
    )
    lap = add_face(
        lap,
        mixed,
        wide_field[:, :, 2 : rows + 2],
        mob_block,
        wide_mob[:, :, 2 : rows + 2],
        (row_ids < all_rows - 1)[:, None],
    )
    for shift_by, valid_cells in (
        (1, column_ids > 0),
        (-1, column_ids < COLS - 1),
        (COLS, cell_ids >= COLS),
        (-COLS, cell_ids < COLS),
    ):
        moved = jnp.roll(mixed, shift_by, axis=3)
        moved_mob = jnp.roll(mob_block, shift_by, axis=3)
        lap = add_face(lap, mixed, moved, mob_block, moved_mob, valid_cells)
    drive = 0.25 * dos[:, None, None]
    out_even = mixed[0] + 0.08 * lap[0] + drive * mixed[1]
    out_odd = mixed[1] + 0.08 * lap[1] - drive * mixed[0]
    return jnp.stack([out_even, out_odd])


def solution(mesh):
    in_specs = (
        P(None, "egrp", "space", None),
        P(None, None, "egrp", "space", None),
        P(None, None, "egrp", "space", None),
        P("space", None),
        P("space", None),
        P(),
        P(),
        P(),
    )
    out_specs = P(None, "egrp", "space", None)
    return jax.shard_map(local, mesh=mesh, in_specs=in_specs, out_specs=out_specs, check_vma=False)
```

profile of v0, /device:TPU:11, one launch (start us, length us, event | category | flops | bytes accessed | tf_op | source)
XLA Modules:
  0.0 195.8 jit_solution(16239742261708099260)
XLA Ops:
  0.0 1.7 fusion.84
  1.7 1.4 copy.175
  3.1 3.8 %all-to-all-start = ((f32[512,2,256]{0,2,1:T(8,128)}), f32[512,2,256]{0,2,1:T(8,128)S(1)}, u32[]{:S(2)}, u32[]{:S(2)}) async-start(f32[512,2,256]{0,2,1:T(8,128)} %bitcast.6), calls=%async_computation | async-start | bytes 2097152 | tf_op jit(solution)/shard_map/all_to_all | solution.py:52
  6.9 4.0 %collective-permute-start = (f32[1,1,1,128]{3,2,1,0:T(1,128)S(1)}, f32[1,1,1,128]{3,2,1,0:T(1,128)S(1)}, u32[]{:S(2)}, u32[]{:S(2)}) collective-permute-start(f32[1,1,1,128]{3,2,1,0:T(1,128)S(1)} %get-tuple-element.53), channel_id=1, source_target_pairs={{0,1},{1,2},{2,3},{3,4},{4,5},{5,6},{6,7},{7,8},{8,9},{9,10},{10,1... | collective-permute-start | bytes 1544 | tf_op jit(solution)/shard_map/ppermute | solution.py:18
  10.9 1.9 collective-permute-start.2
  23.6 5.1 %reshape.555 = bf16[4,2,262144]{2,1,0:T(2,128)(2,1)} reshape(bf16[4,2,512,4,128]{4,3,2,1,0:T(4,128)(2,1)} %param.13) | data formatting | bytes 8388608 | tf_op jit(solution)/shard_map/reshape | solution.py:34
  28.7 4.1 %fusion.83 = (bf16[1,1,512,4,128]{4,3,2,1,0:T(4,128)(2,1)}, bf16[1,1,512,4,128]{4,3,2,1,0:T(4,128)(2,1)}, bf16[1,1,512,4,128]{4,3,2,1,0:T(4,128)(2,1)}, bf16[1,1...) fusion(bf16[4,2,512,4,128]{4,3,2,1,0:T(4,128)(2,1)} %param.13), kind=kLoop, calls=%fused_computation.196 | loop fusion | bytes 8388608 | tf_op jit(solution)/shard_map/slice | solution.py:97
  33.7 2.5 %add_multiply_fusion.2 = (f32[512]{0:T(512)S(1)}, f32[512]{0:T(512)S(1)}) fusion(s32[]{:T(128)} %bitcast.10, f32[]{:T(128)} %bitcast.2, s32[]{:T(128)S(6)} %mul.605, s32[]{:T(128)} %bitcast.9, f32[]{:T(128)} %bitcast.1), kind=kLoop, calls=%fused_computation.143 | loop fusion | flops 17920 | bytes 4116 | tf_op jit(solution)/shard_map/mul | solution.py:49
  36.2 2.5 %add_multiply_fusion = (f32[512]{0:T(512)S(1)}, f32[512]{0:T(512)S(1)}) fusion(s32[]{:T(128)} %bitcast.12, f32[]{:T(128)} %bitcast.4, s32[]{:T(128)S(6)} %mul.605, s32[]{:T(128)} %bitcast.11, f32[]{:T(128)} %bitcast.3), kind=kLoop, calls=%fused_computation.141 | loop fusion | flops 17920 | bytes 4116 | tf_op jit(solution)/shard_map/mul | solution.py:49
  38.7 2.4 %select_select_fusion.2 = (f32[4,128]{1,0:T(4,128)S(1)}, pred[4,128]{1,0:T(4,128)(4,1)S(1)}, pred[4,128]{1,0:T(4,128)(4,1)S(1)}, pred[4,128]{1,0:T(4,128)(4,1)S(1)}, pred[4,128]{1,0:T(4,128)(4,1)S(1)}) fusion(f32[]{:T(128)} %bitcast.4, f32[]{:T(128)} %bitcast.3, f32[]{:T(128)} %bitcast.2, f32[]{:T(128)} %bitcast.1, s32[4,128]{1,0:T(4,128)S(1)} %copy-done.22), kind=kLoop, calls=%fused_computation.163 | loop fusion | flops 4096 | bytes 6160 | tf_op jit(solution)/shard_map/jit(_where)/select_n | solution.py:51
  41.5 4.1 %fusion.82 = (bf16[1,1,512,4,128]{4,3,2,1,0:T(4,128)(2,1)}, bf16[1,1,512,4,128]{4,3,2,1,0:T(4,128)(2,1)}, bf16[1,1,512,4,128]{4,3,2,1,0:T(4,128)(2,1)}, bf16[1,1...) fusion(bf16[4,2,512,4,128]{4,3,2,1,0:T(4,128)(2,1)} %param.12), kind=kLoop, calls=%fused_computation.195 | loop fusion | bytes 8388608 | tf_op jit(solution)/shard_map/slice | solution.py:96
  45.7 2.2 %copy.185 = bf16[1,1,512,4,128]{2,4,3,1,0:T(8,128)(2,1)} copy(bf16[1,1,512,4,128]{4,3,2,1,0:T(4,128)(2,1)} %get-tuple-element.22) | data formatting | bytes 1048576
  47.9 1.1 copy.186
  49.0 2.1 %copy.187 = bf16[1,1,512,4,128]{2,4,3,1,0:T(8,128)(2,1)} copy(bf16[1,1,512,4,128]{4,3,2,1,0:T(4,128)(2,1)} %get-tuple-element.21) | data formatting | bytes 1048576
  51.1 1.1 copy.188
  52.2 2.2 %copy.189 = bf16[1,1,512,4,128]{2,4,3,1,0:T(8,128)(2,1)} copy(bf16[1,1,512,4,128]{4,3,2,1,0:T(4,128)(2,1)} %get-tuple-element.20) | data formatting | bytes 1048576
  54.4 2.2 %copy.190 = bf16[1,1,512,4,128]{2,4,3,1,0:T(8,128)(2,1)} copy(bf16[1,1,512,4,128]{4,3,2,1,0:T(4,128)(2,1)} %get-tuple-element.28) | data formatting | bytes 1048576
  56.6 2.1 %copy.191 = bf16[1,1,512,4,128]{2,4,3,1,0:T(8,128)(2,1)} copy(bf16[1,1,512,4,128]{4,3,2,1,0:T(4,128)(2,1)} %get-tuple-element.26) | data formatting | bytes 1048576
  58.7 1.2 copy.192
  59.8 2.2 %copy.177 = bf16[1,1,512,4,128]{2,4,3,1,0:T(8,128)(2,1)} copy(bf16[1,1,512,4,128]{4,3,2,1,0:T(4,128)(2,1)} %get-tuple-element.19) | data formatting | bytes 1048576
  62.0 1.2 copy.178
  63.2 1.1 copy.179
  65.0 2.3 %fusion.25 = f32[1024,256]{1,0:T(8,128)} fusion(s32[]{:T(128)S(6)} %select_n.228, f32[1024,256]{1,0:T(8,128)S(1)} %bitcast.141, s32[]{:T(128)S(6)} %select_n.229, s32[]{:T(128)S(6)} %select_n.230, s32[]{:T(128)S(6)} %select_n.231, s32[]{:T(128)S(6)} %select_n.232, s32[]{:T(128)S(6)} %select_n.233, s32[]{:T(128)S(6)} %select_n.234, s32[]{:T(128)S(6)} %select_n.235, ...), kind=kLoop, calls=%fused_computation.64 | loop fusion | flops 4194304 | bytes 2098208 | tf_op jit(solution)/shard_map/jit(_where)/select_n | solution.py:66
  67.3 3.8 %all-to-all-start.1 = ((f32[2,512,256]{2,1,0:T(8,128)}), f32[2,512,256]{2,1,0:T(8,128)S(1)}, u32[]{:S(2)}, u32[]{:S(2)}) async-start(f32[2,512,256]{2,1,0:T(8,128)} %bitcast.13), calls=%async_computation.1 | async-start | bytes 2097152 | tf_op jit(solution)/shard_map/all_to_all | solution.py:69
  71.1 9.5 %fusion = f32[2,4,4]{2,1,0:T(4,128)S(1)} fusion(bf16[4,2,262144]{2,1,0:T(2,128)(2,1)} %reshape.555), kind=kOutput, calls=%fused_computation.18 | convolution fusion | flops 16777216 | bytes 4194432 | tf_op jit(solution)/shard_map/dot_general | solution.py:79
  80.6 2.2 %copy.180 = bf16[1,1,512,4,128]{2,4,3,1,0:T(8,128)(2,1)} copy(bf16[1,1,512,4,128]{4,3,2,1,0:T(4,128)(2,1)} %get-tuple-element.33) | data formatting | bytes 1048576
  82.8 2.1 %copy.181 = bf16[1,1,512,4,128]{2,4,3,1,0:T(8,128)(2,1)} copy(bf16[1,1,512,4,128]{4,3,2,1,0:T(4,128)(2,1)} %get-tuple-element.24) | data formatting | bytes 1048576
  84.9 1.1 copy.182
  86.0 2.1 %copy.183 = bf16[1,1,512,4,128]{2,4,3,1,0:T(8,128)(2,1)} copy(bf16[1,1,512,4,128]{4,3,2,1,0:T(4,128)(2,1)} %get-tuple-element.23) | data formatting | bytes 1048576
  88.1 1.1 copy.184
  89.3 1.3 copy.141
  90.6 2.3 %divide_subtract_fusion.1 = (f32[1,512,4,128]{1,3,2,0:T(8,128)S(1)}, f32[1,512,4,128]{1,3,2,0:T(8,128)S(1)}) fusion(f32[1,512,4,128]{1,3,2,0:T(8,128)} %copy.175, f32[1,512,4,128]{1,3,2,0:T(8,128)} %bitcast.146, f32[512]{0:T(512)S(1)} %get-tuple-element.98, f32[512]{0:T(512)S(1)} %get-tuple-element.99, f32[512]{0:T(512)S(1)} %get-tuple-element.100, ...), kind=kLoop, calls=%fused_computation.94 | loop fusion | flops 3407872 | bytes 5257216 | tf_op jit(solution)/shard_map/sub | solution.py:75
  92.9 1.3 copy.142
  94.2 1.3 copy.144
  95.6 1.6 pad_maximum_fusion.5
  97.2 2.9 %copy.145 = f32[2,512,4,128]{3,2,1,0:T(4,128)} copy(f32[2,512,4,128]{1,3,2,0:T(8,128)} %pad_maximum_fusion.5) | data formatting | bytes 4194304 | tf_op jit(solution)/shard_map/stack | solution.py:75
  100.1 5.3 %multiply_reduce_fusion = f32[4,2]{1,0:T(4,128)S(1)} fusion(bf16[4,2,512,4,128]{4,3,2,1,0:T(4,128)(2,1)} %param.13, f32[2,512,4,128]{3,2,1,0:T(4,128)} %copy.145), kind=kLoop, calls=%fused_computation | loop fusion | flops 6291448 | bytes 6291488 | tf_op jit(solution)/shard_map/reduce_sum | solution.py:77
  105.4 2.3 %fusion.15 = f32[2]{0:T(128)S(1)} fusion(f32[1,262144]{1,0:T(1,128)S(1)} %bitcast.143, f32[1,262144]{1,0:T(1,128)S(1)} %bitcast.142), kind=kLoop, calls=%fused_computation.38 | loop fusion | flops 1572862 | bytes 2097160 | tf_op jit(solution)/shard_map/reduce_sum | solution.py:78
  107.7 40.7 %all-reduce.1 = (f32[2,4,4]{2,1,0:T(4,128)S(1)}, f32[2,4]{0,1:T(4,128)S(1)}, f32[2]{0:T(128)S(1)}) all-reduce(f32[2,4,4]{2,1,0:T(4,128)S(1)} %fusion, f32[2,4]{0,1:T(4,128)S(1)} %bitcast.152, f32[2]{0:T(128)S(1)} %fusion.15), channel_id=1, replica_groups=mesh['egrp'=2,'space'=16] {'egrp','space'}, use_global_device_ids=true, to_apply=%region_4.5 | all-reduce | flops 42 | bytes 336 | tf_op jit(solution)/shard_map/psum | solution.py:82
  152.8 0.8 fusion.92
  160.6 6.4 %bitcast_add_fusion = f32[1,512,4,128]{1,3,2,0:T(8,128)S(1)} fusion(bf16[1,1,512,4,128]{2,4,3,1,0:T(8,128)(2,1)} %copy.192, bf16[1,1,512,4,128]{2,4,3,1,0:T(8,128)(2,1)} %copy.191, bf16[1,1,512,4,128]{2,4,3,1,0:T(8,128)(2,1)} %copy.190, bf16[1,1,512,4,128]{2,4,3,1,0:T(8,128)(2,1)} %copy.189, bf16[1,1,512,4,128]{2,4,3,1,0:T(8,128)(2,1)} %copy.188, ...), kind=kLoop, calls=%fused_computation.86 | loop fusion | flops 9175040 | bytes 6303764 | tf_op jit(solution)/shard_map/add | solution.py:95
  167.1 5.4 %bitcast_add_fusion.4 = f32[1,512,4,128]{1,3,2,0:T(8,128)S(1)} fusion(bf16[1,1,512,4,128]{2,4,3,1,0:T(8,128)(2,1)S(1)} %copy-done.18, bf16[1,1,512,4,128]{2,4,3,1,0:T(8,128)(2,1)S(1)} %copy-done.17, bf16[1,1,512,4,128]{2,4,3,1,0:T(8,128)(2,1)S(1)} %copy-done.16, bf16[1,1,512,4,128]{2,4,3,1,0:T(8,128)(2,1)S(1)} %copy-done.15, ...), kind=kLoop, calls=%fused_computation.90 | loop fusion | flops 7077888 | bytes 7340052 | tf_op jit(solution)/shard_map/add | solution.py:95
  172.5 4.5 %collective-permute-start.1 = (f32[2,512,1,128]{1,3,2,0:T(8,128)S(1)}, f32[2,512,1,128]{1,3,2,0:T(8,128)S(1)}, u32[]{:S(2)}, u32[]{:S(2)}) collective-permute-start(f32[2,512,1,128]{1,3,2,0:T(8,128)S(1)} %get-tuple-element.41), channel_id=1, source_target_pairs={{0,1},{1,2},{2,3},{3,4},{4,5},{5,6},{6,7},{7,8},{8,9},{9,10},{10,1... | collective-permute-start | bytes 1572872 | tf_op jit(solution)/shard_map/ppermute | solution.py:18
  177.0 1.9 collective-permute-start.3
  179.7 9.0 %collective-permute-done.1 = f32[2,512,1,128]{1,3,2,0:T(8,128)S(1)} collective-permute-done((f32[2,512,1,128]{1,3,2,0:T(8,128)S(1)}, f32[2,512,1,128]{1,3,2,0:T(8,128)S(1)}, u32[]{:S(2)}, u32[]{:S(2)}) %collective-permute-start.1) | collective-permute-done | bytes 524320 | tf_op jit(solution)/shard_map/ppermute | solution.py:18
  188.7 1.6 collective-permute-done.3
  190.3 2.9 %fusion.11 = f32[2,512,4,128]{1,3,2,0:T(8,128)S(1)} fusion(f32[2,512,1,128]{1,3,2,0:T(8,128)S(1)} %collective-permute-done.3, f32[1,512,4,128]{1,3,2,0:T(8,128)S(1)} %bitcast_add_fusion, f32[1,512,4,128]{1,3,2,0:T(8,128)S(1)} %bitcast_add_fusion.4, f32[2,512,1,128]{1,3,2,0:T(8,128)S(1)} %collective-permute-done.1, ...), kind=kLoop, calls=%fused_computation.30 | loop fusion | flops 15204352 | bytes 11545096 | tf_op jit(solution)/shard_map/add | solution.py:27
  194.0 1.8 copy.174
  (109 shorter events, 15.5 us)
Async XLA Ops:
  1.7 5.3 %copy-start.19 = (f32[4,128]{1,0:T(4,128)S(1)}, f32[4,128]{1,0:T(4,128)}, u32[]{:S(2)}) copy-start(f32[4,128]{1,0:T(4,128)} %param.14) | copy-start | bytes 6148
  1.7 11.2 %copy-start.20 = (s32[4]{0:T(128)S(1)}, s32[4]{0:T(128)}, u32[]{:S(2)}) copy-start(s32[4]{0:T(128)} %param.16) | copy-start | bytes 52
  3.1 61.6 %all-to-all-start = ((f32[512,2,256]{0,2,1:T(8,128)}), f32[512,2,256]{0,2,1:T(8,128)S(1)}, u32[]{:S(2)}, u32[]{:S(2)}) async-start(f32[512,2,256]{0,2,1:T(8,128)} %bitcast.6), calls=%async_computation | async-start | bytes 2097152 | tf_op jit(solution)/shard_map/all_to_all | solution.py:52
  6.9 82.3 %collective-permute-start = (f32[1,1,1,128]{3,2,1,0:T(1,128)S(1)}, f32[1,1,1,128]{3,2,1,0:T(1,128)S(1)}, u32[]{:S(2)}, u32[]{:S(2)}) collective-permute-start(f32[1,1,1,128]{3,2,1,0:T(1,128)S(1)} %get-tuple-element.53), channel_id=1, source_target_pairs={{0,1},{1,2},{2,3},{3,4},{4,5},{5,6},{6,7},{7,8},{8,9},{9,10},{10,1... | collective-permute-start | bytes 1544 | tf_op jit(solution)/shard_map/ppermute | solution.py:18
  10.9 78.3 %collective-permute-start.2 = (f32[1,1,1,128]{3,2,1,0:T(1,128)S(1)}, f32[1,1,1,128]{3,2,1,0:T(1,128)S(1)}, u32[]{:S(2)}, u32[]{:S(2)}) collective-permute-start(f32[1,1,1,128]{3,2,1,0:T(1,128)S(1)} %get-tuple-element.54), channel_id=1, source_target_pairs={{1,0},{2,1},{3,2},{4,3},{5,4},{6,5},{7,6},{8,7},{9,8},{10,9},{11,1... | collective-permute-start | bytes 1544 | tf_op jit(solution)/shard_map/ppermute | solution.py:21
  28.7 4.3 %copy-start.21 = (f32[4]{0:T(128)S(1)}, f32[4]{0:T(128)}, u32[]{:S(2)}) copy-start(f32[4]{0:T(128)} %param.17) | copy-start | bytes 52
  28.7 10.0 %copy-start.22 = (s32[4,128]{1,0:T(4,128)S(1)}, s32[4,128]{1,0:T(4,128)}, u32[]{:S(2)}) copy-start(s32[4,128]{1,0:T(4,128)} %param.15) | copy-start | bytes 6148
  32.8 8.7 %copy-start.23 = (s32[2,4]{1,0:T(2,128)S(1)}, s32[2,4]{1,0:T(2,128)}, u32[]{:S(2)}) copy-start(s32[2,4]{1,0:T(2,128)} %param.18) | copy-start | bytes 100
  41.5 6.3 %copy-start.7 = (bf16[1,1,512,4,128]{4,3,2,1,0:T(4,128)(2,1)S(1)}, bf16[1,1,512,4,128]{4,3,2,1,0:T(4,128)(2,1)}, u32[]{:S(2)}) copy-start(bf16[1,1,512,4,128]{4,3,2,1,0:T(4,128)(2,1)} %get-tuple-element.30) | copy-start | bytes 1572868
  45.7 5.4 %copy-start.6 = (bf16[1,1,512,4,128]{4,3,2,1,0:T(4,128)(2,1)S(1)}, bf16[1,1,512,4,128]{4,3,2,1,0:T(4,128)(2,1)}, u32[]{:S(2)}) copy-start(bf16[1,1,512,4,128]{4,3,2,1,0:T(4,128)(2,1)} %get-tuple-element.29) | copy-start | bytes 1572868
  51.1 7.6 %copy-start.5 = (bf16[1,1,512,4,128]{4,3,2,1,0:T(4,128)(2,1)S(1)}, bf16[1,1,512,4,128]{4,3,2,1,0:T(4,128)(2,1)}, u32[]{:S(2)}) copy-start(bf16[1,1,512,4,128]{4,3,2,1,0:T(4,128)(2,1)} %get-tuple-element.34) | copy-start | bytes 1572868
  54.4 7.7 %copy-start.4 = (bf16[1,1,512,4,128]{4,3,2,1,0:T(4,128)(2,1)S(1)}, bf16[1,1,512,4,128]{4,3,2,1,0:T(4,128)(2,1)}, u32[]{:S(2)}) copy-start(bf16[1,1,512,4,128]{4,3,2,1,0:T(4,128)(2,1)} %get-tuple-element.27) | copy-start | bytes 1572868
  59.8 3.4 %copy-start.8 = (bf16[1,1,512,4,128]{4,3,2,1,0:T(4,128)(2,1)S(1)}, bf16[1,1,512,4,128]{4,3,2,1,0:T(4,128)(2,1)}, u32[]{:S(2)}) copy-start(bf16[1,1,512,4,128]{4,3,2,1,0:T(4,128)(2,1)} %get-tuple-element.25) | copy-start | bytes 1572868
  67.3 22.0 %all-to-all-start.1 = ((f32[2,512,256]{2,1,0:T(8,128)}), f32[2,512,256]{2,1,0:T(8,128)S(1)}, u32[]{:S(2)}, u32[]{:S(2)}) async-start(f32[2,512,256]{2,1,0:T(8,128)} %bitcast.13), calls=%async_computation.1 | async-start | bytes 2097152 | tf_op jit(solution)/shard_map/all_to_all | solution.py:69
  80.6 4.3 %copy-start.3 = (bf16[1,1,512,4,128]{4,3,2,1,0:T(4,128)(2,1)S(1)}, bf16[1,1,512,4,128]{4,3,2,1,0:T(4,128)(2,1)}, u32[]{:S(2)}) copy-start(bf16[1,1,512,4,128]{4,3,2,1,0:T(4,128)(2,1)} %get-tuple-element.32) | copy-start | bytes 1572868
  80.6 7.5 %copy-start.2 = (bf16[1,1,512,4,128]{4,3,2,1,0:T(4,128)(2,1)S(1)}, bf16[1,1,512,4,128]{4,3,2,1,0:T(4,128)(2,1)}, u32[]{:S(2)}) copy-start(bf16[1,1,512,4,128]{4,3,2,1,0:T(4,128)(2,1)} %get-tuple-element.31) | copy-start | bytes 1572868
  100.1 5.3 %copy-start = (f32[1,512,4,128]{3,2,1,0:T(4,128)S(1)}, f32[1,512,4,128]{3,2,1,0:T(4,128)}, u32[]{:S(2)}) copy-start(f32[1,512,4,128]{3,2,1,0:T(4,128)} %copy.142) | copy-start | bytes 3145732
  100.1 5.3 %copy-start.1 = (f32[1,512,4,128]{3,2,1,0:T(4,128)S(1)}, f32[1,512,4,128]{3,2,1,0:T(4,128)}, u32[]{:S(2)}) copy-start(f32[1,512,4,128]{3,2,1,0:T(4,128)} %copy.144) | copy-start | bytes 3145732
  105.4 55.1 %copy-start.9 = (bf16[1,1,512,4,128]{2,4,3,1,0:T(8,128)(2,1)S(1)}, bf16[1,1,512,4,128]{2,4,3,1,0:T(8,128)(2,1)}, u32[]{:S(2)}) copy-start(bf16[1,1,512,4,128]{2,4,3,1,0:T(8,128)(2,1)} %copy.185) | copy-start | bytes 1572868
  105.4 55.1 %copy-start.11 = (bf16[1,1,512,4,128]{2,4,3,1,0:T(8,128)(2,1)S(1)}, bf16[1,1,512,4,128]{2,4,3,1,0:T(8,128)(2,1)}, u32[]{:S(2)}) copy-start(bf16[1,1,512,4,128]{2,4,3,1,0:T(8,128)(2,1)} %copy.186) | copy-start | bytes 1572868
  160.6 6.4 %copy-start.10 = (bf16[1,1,512,4,128]{2,4,3,1,0:T(8,128)(2,1)S(1)}, bf16[1,1,512,4,128]{2,4,3,1,0:T(8,128)(2,1)}, u32[]{:S(2)}) copy-start(bf16[1,1,512,4,128]{2,4,3,1,0:T(8,128)(2,1)} %copy.177) | copy-start | bytes 1572868
  160.6 6.4 %copy-start.12 = (bf16[1,1,512,4,128]{2,4,3,1,0:T(8,128)(2,1)S(1)}, bf16[1,1,512,4,128]{2,4,3,1,0:T(8,128)(2,1)}, u32[]{:S(2)}) copy-start(bf16[1,1,512,4,128]{2,4,3,1,0:T(8,128)(2,1)} %copy.178) | copy-start | bytes 1572868
  160.6 6.4 %copy-start.13 = (bf16[1,1,512,4,128]{2,4,3,1,0:T(8,128)(2,1)S(1)}, bf16[1,1,512,4,128]{2,4,3,1,0:T(8,128)(2,1)}, u32[]{:S(2)}) copy-start(bf16[1,1,512,4,128]{2,4,3,1,0:T(8,128)(2,1)} %copy.179) | copy-start | bytes 1572868
  160.6 6.4 %copy-start.14 = (bf16[1,1,512,4,128]{2,4,3,1,0:T(8,128)(2,1)S(1)}, bf16[1,1,512,4,128]{2,4,3,1,0:T(8,128)(2,1)}, u32[]{:S(2)}) copy-start(bf16[1,1,512,4,128]{2,4,3,1,0:T(8,128)(2,1)} %copy.180) | copy-start | bytes 1572868
  160.6 6.4 %copy-start.15 = (bf16[1,1,512,4,128]{2,4,3,1,0:T(8,128)(2,1)S(1)}, bf16[1,1,512,4,128]{2,4,3,1,0:T(8,128)(2,1)}, u32[]{:S(2)}) copy-start(bf16[1,1,512,4,128]{2,4,3,1,0:T(8,128)(2,1)} %copy.181) | copy-start | bytes 1572868
  160.6 6.4 %copy-start.16 = (bf16[1,1,512,4,128]{2,4,3,1,0:T(8,128)(2,1)S(1)}, bf16[1,1,512,4,128]{2,4,3,1,0:T(8,128)(2,1)}, u32[]{:S(2)}) copy-start(bf16[1,1,512,4,128]{2,4,3,1,0:T(8,128)(2,1)} %copy.182) | copy-start | bytes 1572868
  160.6 6.4 %copy-start.17 = (bf16[1,1,512,4,128]{2,4,3,1,0:T(8,128)(2,1)S(1)}, bf16[1,1,512,4,128]{2,4,3,1,0:T(8,128)(2,1)}, u32[]{:S(2)}) copy-start(bf16[1,1,512,4,128]{2,4,3,1,0:T(8,128)(2,1)} %copy.183) | copy-start | bytes 1572868
  160.6 6.4 %copy-start.18 = (bf16[1,1,512,4,128]{2,4,3,1,0:T(8,128)(2,1)S(1)}, bf16[1,1,512,4,128]{2,4,3,1,0:T(8,128)(2,1)}, u32[]{:S(2)}) copy-start(bf16[1,1,512,4,128]{2,4,3,1,0:T(8,128)(2,1)} %copy.184) | copy-start | bytes 1572868
  172.5 16.2 %collective-permute-start.1 = (f32[2,512,1,128]{1,3,2,0:T(8,128)S(1)}, f32[2,512,1,128]{1,3,2,0:T(8,128)S(1)}, u32[]{:S(2)}, u32[]{:S(2)}) collective-permute-start(f32[2,512,1,128]{1,3,2,0:T(8,128)S(1)} %get-tuple-element.41), channel_id=1, source_target_pairs={{0,1},{1,2},{2,3},{3,4},{4,5},{5,6},{6,7},{7,8},{8,9},{9,10},{10,1... | collective-permute-start | bytes 1572872 | tf_op jit(solution)/shard_map/ppermute | solution.py:18
  177.0 13.3 %collective-permute-start.3 = (f32[2,512,1,128]{1,3,2,0:T(8,128)S(1)}, f32[2,512,1,128]{1,3,2,0:T(8,128)S(1)}, u32[]{:S(2)}, u32[]{:S(2)}) collective-permute-start(f32[2,512,1,128]{1,3,2,0:T(8,128)S(1)} %get-tuple-element.42), channel_id=1, source_target_pairs={{1,0},{2,1},{3,2},{4,3},{5,4},{6,5},{7,6},{8,7},{9,8},{10,9},{11,1... | collective-permute-start | bytes 1572872 | tf_op jit(solution)/shard_map/ppermute | solution.py:21
where the time goes:
time: 197 us; the launch traced here: 196 us
  local copies, waits for them, and re-layouts  57.4 us (29%)
  other arithmetic  45.2 us (23%)
  blocking collectives  40.7 us (21%)
  starting transfers between devices  19.9 us (10%)
  matrix products  11.5 us (6%)
  waiting for transfers between devices  10.6 us (5%)
  between operations  10.6 us (5%)
    psum x1, blocking collectives, local(): lax.psum((among, cross, self_term), ('egrp', 'space'))  40.7 us
    unnamed x66, local copies, waits for them, and re-layouts  29.2 us
    add x2, other arithmetic, local(): part_mix + coeffs[index + 1] * (hist_x[index, field].astype(jnp.float32)...  11.7 us
    dot_general x1, matrix products, local(): lax.dot_general(flat_g, flat_g, (((2,), (2,)), ((1,), (1,))), preferred_e...  9.54 us
    ppermute x2, waiting for transfers between devices, extended(): lax.ppermute(lax.slice_in_dim(block, block.shape[dim] - width, None, axis...  9 us
    ppermute x2, starting transfers between devices, extended(): lax.ppermute(lax.slice_in_dim(block, block.shape[dim] - width, None, axis...  8.46 us
    reduce_sum x1, other arithmetic, local(): jnp.sum(flat_g.astype(jnp.float32) * res_flat[None], axis=2)  5.32 us
    reshape x1, local copies, waits for them, and re-layouts, local(): flat_g = hist_g.reshape(HISTORY, 2, -1)  5.11 us
  transfers between devices with their start and end apart: 6, of which 2 were waited for; matrix products, arithmetic and copies ran while one was open for 32% of the time, Pallas kernels for 0%

commit v1 on v0

--- a/solution.py
+++ b/solution.py
@@ -79,7 +79,7 @@
     among = lax.dot_general(
         flat_g, flat_g, (((2,), (2,)), ((1,), (1,))), preferred_element_type=jnp.float32
     )
-    among, cross, self_term = lax.psum((among, cross, self_term), ("egrp", "space"))
+    among, cross, self_term = lax.psum(lax.psum((among, cross, self_term), "space"), "egrp")
     fields = []
     for field in range(2):
         top = jnp.concatenate([self_term[field][None], cross[field]])[None, :]

time: 197 us -> 187 us (0.949)
  the two profiles are of different devices: /device:TPU:11 before, /device:TPU:6 now
where the time goes in v1:
time: 187 us; the launch traced here: 186 us
  local copies, waits for them, and re-layouts  57.4 us (31%)
  other arithmetic  45.1 us (24%)
  blocking collectives  33.4 us (18%)
  starting transfers between devices  19 us (10%)
  matrix products  11.4 us (6%)
  between operations  10.1 us (5%)
  waiting for transfers between devices  9.76 us (5%)
    unnamed x66, local copies, waits for them, and re-layouts  29.2 us
    psum x1, blocking collectives, local(): lax.psum((among, cross, self_term), 'space')  28.4 us
    add x2, other arithmetic, local(): part_mix + coeffs[index + 1] * (hist_x[index, field].astype(jnp.float32)...  11.7 us
    ppermute x2, waiting for transfers between devices, extended(): lax.ppermute(lax.slice_in_dim(block, block.shape[dim] - width, None, axis...  9.75 us
    dot_general x1, matrix products, local(): lax.dot_general(flat_g, flat_g, (((2,), (2,)), ((1,), (1,))), preferred_e...  9.54 us
    ppermute x2, starting transfers between devices, extended(): lax.ppermute(lax.slice_in_dim(block, 0, width, axis=dim), axis, backward)  7.28 us
    reduce_sum x1, other arithmetic, local(): jnp.sum(flat_g.astype(jnp.float32) * res_flat[None], axis=2)  5.32 us
    reshape x1, local copies, waits for them, and re-layouts, local(): flat_g = hist_g.reshape(HISTORY, 2, -1)  5.1 us
  transfers between devices with their start and end apart: 6, of which 1 were waited for; matrix products, arithmetic and copies ran while one was open for 34% of the time, Pallas kernels for 0%

profile of v1, /device:TPU:6, one launch (start us, length us, event | category | flops | bytes accessed | tf_op | source)
XLA Modules:
  0.0 186.2 jit_solution(14561547262903860062)
XLA Ops:
  0.0 1.7 fusion.84
  1.7 1.4 copy.175
  3.1 4.1 %all-to-all-start = ((f32[512,2,256]{0,2,1:T(8,128)}), f32[512,2,256]{0,2,1:T(8,128)S(1)}, u32[]{:S(2)}, u32[]{:S(2)}) async-start(f32[512,2,256]{0,2,1:T(8,128)} %bitcast.6), calls=%async_computation | async-start | bytes 2097152 | tf_op jit(solution)/shard_map/all_to_all | solution.py:52
  7.2 1.9 %collective-permute-start = (f32[1,1,1,128]{3,2,1,0:T(1,128)S(1)}, f32[1,1,1,128]{3,2,1,0:T(1,128)S(1)}, u32[]{:S(2)}, u32[]{:S(2)}) collective-permute-start(f32[1,1,1,128]{3,2,1,0:T(1,128)S(1)} %get-tuple-element.56), channel_id=1, source_target_pairs={{0,1},{1,2},{2,3},{3,4},{4,5},{5,6},{6,7},{7,8},{8,9},{9,10},{10,1... | collective-permute-start | bytes 1544 | tf_op jit(solution)/shard_map/ppermute | solution.py:18
  9.1 3.6 %collective-permute-start.2 = (f32[1,1,1,128]{3,2,1,0:T(1,128)S(1)}, f32[1,1,1,128]{3,2,1,0:T(1,128)S(1)}, u32[]{:S(2)}, u32[]{:S(2)}) collective-permute-start(f32[1,1,1,128]{3,2,1,0:T(1,128)S(1)} %get-tuple-element.57), channel_id=1, source_target_pairs={{1,0},{2,1},{3,2},{4,3},{5,4},{6,5},{7,6},{8,7},{9,8},{10,9},{11,1... | collective-permute-start | bytes 1544 | tf_op jit(solution)/shard_map/ppermute | solution.py:21
  22.9 5.1 %reshape.555 = bf16[4,2,262144]{2,1,0:T(2,128)(2,1)} reshape(bf16[4,2,512,4,128]{4,3,2,1,0:T(4,128)(2,1)} %param.13) | data formatting | bytes 8388608 | tf_op jit(solution)/shard_map/reshape | solution.py:34
  28.0 4.1 %fusion.83 = (bf16[1,1,512,4,128]{4,3,2,1,0:T(4,128)(2,1)}, bf16[1,1,512,4,128]{4,3,2,1,0:T(4,128)(2,1)}, bf16[1,1,512,4,128]{4,3,2,1,0:T(4,128)(2,1)}, bf16[1,1...) fusion(bf16[4,2,512,4,128]{4,3,2,1,0:T(4,128)(2,1)} %param.13), kind=kLoop, calls=%fused_computation.196 | loop fusion | bytes 8388608 | tf_op jit(solution)/shard_map/slice | solution.py:97
  33.1 2.5 %add_multiply_fusion = (f32[512]{0:T(512)S(1)}, f32[512]{0:T(512)S(1)}) fusion(s32[]{:T(128)} %bitcast.12, f32[]{:T(128)} %bitcast.4, s32[]{:T(128)S(6)} %mul.605, s32[]{:T(128)} %bitcast.11, f32[]{:T(128)} %bitcast.3), kind=kLoop, calls=%fused_computation.141 | loop fusion | flops 17920 | bytes 4116 | tf_op jit(solution)/shard_map/mul | solution.py:49
  35.6 2.5 %add_multiply_fusion.2 = (f32[512]{0:T(512)S(1)}, f32[512]{0:T(512)S(1)}) fusion(s32[]{:T(128)} %bitcast.10, f32[]{:T(128)} %bitcast.2, s32[]{:T(128)S(6)} %mul.605, s32[]{:T(128)} %bitcast.9, f32[]{:T(128)} %bitcast.1), kind=kLoop, calls=%fused_computation.143 | loop fusion | flops 17920 | bytes 4116 | tf_op jit(solution)/shard_map/mul | solution.py:49
  38.1 2.6 %select_select_fusion.2 = (f32[4,128]{1,0:T(4,128)S(1)}, pred[4,128]{1,0:T(4,128)(4,1)S(1)}, pred[4,128]{1,0:T(4,128)(4,1)S(1)}, pred[4,128]{1,0:T(4,128)(4,1)S(1)}, pred[4,128]{1,0:T(4,128)(4,1)S(1)}) fusion(f32[]{:T(128)} %bitcast.4, f32[]{:T(128)} %bitcast.3, f32[]{:T(128)} %bitcast.2, f32[]{:T(128)} %bitcast.1, s32[4,128]{1,0:T(4,128)S(1)} %copy-done.22), kind=kLoop, calls=%fused_computation.163 | loop fusion | flops 4096 | bytes 6160 | tf_op jit(solution)/shard_map/jit(_where)/select_n | solution.py:51
  41.1 4.1 %fusion.82 = (bf16[1,1,512,4,128]{4,3,2,1,0:T(4,128)(2,1)}, bf16[1,1,512,4,128]{4,3,2,1,0:T(4,128)(2,1)}, bf16[1,1,512,4,128]{4,3,2,1,0:T(4,128)(2,1)}, bf16[1,1...) fusion(bf16[4,2,512,4,128]{4,3,2,1,0:T(4,128)(2,1)} %param.12), kind=kLoop, calls=%fused_computation.195 | loop fusion | bytes 8388608 | tf_op jit(solution)/shard_map/slice | solution.py:96
  45.2 2.2 %copy.185 = bf16[1,1,512,4,128]{2,4,3,1,0:T(8,128)(2,1)} copy(bf16[1,1,512,4,128]{4,3,2,1,0:T(4,128)(2,1)} %get-tuple-element.25) | data formatting | bytes 1048576
  47.4 1.1 copy.186
  48.5 2.1 %copy.187 = bf16[1,1,512,4,128]{2,4,3,1,0:T(8,128)(2,1)} copy(bf16[1,1,512,4,128]{4,3,2,1,0:T(4,128)(2,1)} %get-tuple-element.24) | data formatting | bytes 1048576
  50.6 1.1 copy.188
  51.8 2.2 %copy.189 = bf16[1,1,512,4,128]{2,4,3,1,0:T(8,128)(2,1)} copy(bf16[1,1,512,4,128]{4,3,2,1,0:T(4,128)(2,1)} %get-tuple-element.23) | data formatting | bytes 1048576
  53.9 2.2 %copy.190 = bf16[1,1,512,4,128]{2,4,3,1,0:T(8,128)(2,1)} copy(bf16[1,1,512,4,128]{4,3,2,1,0:T(4,128)(2,1)} %get-tuple-element.31) | data formatting | bytes 1048576
  56.1 2.1 %copy.191 = bf16[1,1,512,4,128]{2,4,3,1,0:T(8,128)(2,1)} copy(bf16[1,1,512,4,128]{4,3,2,1,0:T(4,128)(2,1)} %get-tuple-element.29) | data formatting | bytes 1048576
  58.3 1.2 copy.192
  59.4 2.2 %copy.177 = bf16[1,1,512,4,128]{2,4,3,1,0:T(8,128)(2,1)} copy(bf16[1,1,512,4,128]{4,3,2,1,0:T(4,128)(2,1)} %get-tuple-element.22) | data formatting | bytes 1048576
  61.6 1.2 copy.178
  62.8 1.1 copy.179
  64.6 2.3 %fusion.25 = f32[1024,256]{1,0:T(8,128)} fusion(s32[]{:T(128)S(6)} %select_n.228, f32[1024,256]{1,0:T(8,128)S(1)} %bitcast.141, s32[]{:T(128)S(6)} %select_n.229, s32[]{:T(128)S(6)} %select_n.230, s32[]{:T(128)S(6)} %select_n.231, s32[]{:T(128)S(6)} %select_n.232, s32[]{:T(128)S(6)} %select_n.233, s32[]{:T(128)S(6)} %select_n.234, s32[]{:T(128)S(6)} %select_n.235, ...), kind=kLoop, calls=%fused_computation.64 | loop fusion | flops 4194304 | bytes 2098208 | tf_op jit(solution)/shard_map/jit(_where)/select_n | solution.py:66
  66.9 3.8 %all-to-all-start.1 = ((f32[2,512,256]{2,1,0:T(8,128)}), f32[2,512,256]{2,1,0:T(8,128)S(1)}, u32[]{:S(2)}, u32[]{:S(2)}) async-start(f32[2,512,256]{2,1,0:T(8,128)} %bitcast.13), calls=%async_computation.1 | async-start | bytes 2097152 | tf_op jit(solution)/shard_map/all_to_all | solution.py:69
  70.6 9.5 %fusion = f32[2,4,4]{2,1,0:T(4,128)S(1)} fusion(bf16[4,2,262144]{2,1,0:T(2,128)(2,1)} %reshape.555), kind=kOutput, calls=%fused_computation.18 | convolution fusion | flops 16777216 | bytes 4194432 | tf_op jit(solution)/shard_map/dot_general | solution.py:79
  80.2 2.2 %copy.180 = bf16[1,1,512,4,128]{2,4,3,1,0:T(8,128)(2,1)} copy(bf16[1,1,512,4,128]{4,3,2,1,0:T(4,128)(2,1)} %get-tuple-element.36) | data formatting | bytes 1048576
  82.4 2.1 %copy.181 = bf16[1,1,512,4,128]{2,4,3,1,0:T(8,128)(2,1)} copy(bf16[1,1,512,4,128]{4,3,2,1,0:T(4,128)(2,1)} %get-tuple-element.27) | data formatting | bytes 1048576
  84.5 1.1 copy.182
  85.6 2.1 %copy.183 = bf16[1,1,512,4,128]{2,4,3,1,0:T(8,128)(2,1)} copy(bf16[1,1,512,4,128]{4,3,2,1,0:T(4,128)(2,1)} %get-tuple-element.26) | data formatting | bytes 1048576
  87.7 1.1 copy.184
  88.9 1.3 copy.141
  90.2 2.3 %divide_subtract_fusion.1 = (f32[1,512,4,128]{1,3,2,0:T(8,128)S(1)}, f32[1,512,4,128]{1,3,2,0:T(8,128)S(1)}) fusion(f32[1,512,4,128]{1,3,2,0:T(8,128)} %copy.175, f32[1,512,4,128]{1,3,2,0:T(8,128)} %bitcast.146, f32[512]{0:T(512)S(1)} %get-tuple-element.101, f32[512]{0:T(512)S(1)} %get-tuple-element.102, f32[512]{0:T(512)S(1)} %get-tuple-element.103, ...), kind=kLoop, calls=%fused_computation.94 | loop fusion | flops 3407872 | bytes 5257216 | tf_op jit(solution)/shard_map/sub | solution.py:75
  92.5 1.3 copy.142
  93.8 1.3 copy.144
  95.1 1.6 pad_maximum_fusion.5
  96.7 2.9 %copy.145 = f32[2,512,4,128]{3,2,1,0:T(4,128)} copy(f32[2,512,4,128]{1,3,2,0:T(8,128)} %pad_maximum_fusion.5) | data formatting | bytes 4194304 | tf_op jit(solution)/shard_map/stack | solution.py:75
  99.7 5.3 %multiply_reduce_fusion = f32[4,2]{1,0:T(4,128)S(1)} fusion(bf16[4,2,512,4,128]{4,3,2,1,0:T(4,128)(2,1)} %param.13, f32[2,512,4,128]{3,2,1,0:T(4,128)} %copy.145), kind=kLoop, calls=%fused_computation | loop fusion | flops 6291448 | bytes 6291488 | tf_op jit(solution)/shard_map/reduce_sum | solution.py:77
  105.0 2.3 %fusion.15 = f32[2]{0:T(128)S(1)} fusion(f32[1,262144]{1,0:T(1,128)S(1)} %bitcast.143, f32[1,262144]{1,0:T(1,128)S(1)} %bitcast.142), kind=kLoop, calls=%fused_computation.38 | loop fusion | flops 1572862 | bytes 2097160 | tf_op jit(solution)/shard_map/reduce_sum | solution.py:78
  107.3 28.4 %all-reduce.1 = (f32[2,4,4]{2,1,0:T(4,128)S(1)}, f32[2,4]{0,1:T(4,128)S(1)}, f32[2]{0:T(128)S(1)}) all-reduce(f32[2,4,4]{2,1,0:T(4,128)S(1)} %fusion, f32[2,4]{0,1:T(4,128)S(1)} %bitcast.152, f32[2]{0:T(128)S(1)} %fusion.15), channel_id=1, replica_groups=mesh['egrp'=2,'space'=16] {'space'}, use_global_device_ids=true, to_apply=%region_6.7 | all-reduce | flops 42 | bytes 336 | tf_op jit(solution)/shard_map/psum | solution.py:82
  135.7 5.0 %all-reduce.2 = (f32[2,4,4]{2,1,0:T(4,128)S(1)}, f32[2,4]{0,1:T(4,128)S(1)}, f32[2]{0:T(128)S(1)}) all-reduce(f32[2,4,4]{2,1,0:T(4,128)S(1)} %get-tuple-element.9, f32[2,4]{0,1:T(4,128)S(1)} %get-tuple-element.10, f32[2]{0:T(128)S(1)} %get-tuple-element.11), channel_id=1, replica_groups=mesh['egrp'=2,'space'=16] {'egrp'}, use_global_device_ids=true, to_apply=%region_7.8 | all-reduce | flops 42 | bytes 336 | tf_op jit(solution)/shard_map/psum | solution.py:82
  150.5 0.8 fusion.91
  152.7 6.4 %bitcast_add_fusion = f32[1,512,4,128]{1,3,2,0:T(8,128)S(1)} fusion(bf16[1,1,512,4,128]{2,4,3,1,0:T(8,128)(2,1)} %copy.192, bf16[1,1,512,4,128]{2,4,3,1,0:T(8,128)(2,1)} %copy.191, bf16[1,1,512,4,128]{2,4,3,1,0:T(8,128)(2,1)} %copy.190, bf16[1,1,512,4,128]{2,4,3,1,0:T(8,128)(2,1)} %copy.189, bf16[1,1,512,4,128]{2,4,3,1,0:T(8,128)(2,1)} %copy.188, ...), kind=kLoop, calls=%fused_computation.86 | loop fusion | flops 9175040 | bytes 6303764 | tf_op jit(solution)/shard_map/add | solution.py:95
  159.2 5.2 %bitcast_add_fusion.4 = f32[1,512,4,128]{1,3,2,0:T(8,128)S(1)} fusion(bf16[1,1,512,4,128]{2,4,3,1,0:T(8,128)(2,1)S(1)} %copy-done.18, bf16[1,1,512,4,128]{2,4,3,1,0:T(8,128)(2,1)S(1)} %copy-done.17, bf16[1,1,512,4,128]{2,4,3,1,0:T(8,128)(2,1)S(1)} %copy-done.16, bf16[1,1,512,4,128]{2,4,3,1,0:T(8,128)(2,1)S(1)} %copy-done.15, ...), kind=kLoop, calls=%fused_computation.90 | loop fusion | flops 7077888 | bytes 7340052 | tf_op jit(solution)/shard_map/add | solution.py:95
  164.5 1.9 %collective-permute-start.1 = (f32[2,512,1,128]{1,3,2,0:T(8,128)S(1)}, f32[2,512,1,128]{1,3,2,0:T(8,128)S(1)}, u32[]{:S(2)}, u32[]{:S(2)}) collective-permute-start(f32[2,512,1,128]{1,3,2,0:T(8,128)S(1)} %get-tuple-element.44), channel_id=1, source_target_pairs={{0,1},{1,2},{2,3},{3,4},{4,5},{5,6},{6,7},{7,8},{8,9},{9,10},{10,1... | collective-permute-start | bytes 1572872 | tf_op jit(solution)/shard_map/ppermute | solution.py:18
  166.4 3.6 %collective-permute-start.3 = (f32[2,512,1,128]{1,3,2,0:T(8,128)S(1)}, f32[2,512,1,128]{1,3,2,0:T(8,128)S(1)}, u32[]{:S(2)}, u32[]{:S(2)}) collective-permute-start(f32[2,512,1,128]{1,3,2,0:T(8,128)S(1)} %get-tuple-element.45), channel_id=1, source_target_pairs={{1,0},{2,1},{3,2},{4,3},{5,4},{6,5},{7,6},{8,7},{9,8},{10,9},{11,1... | collective-permute-start | bytes 1572872 | tf_op jit(solution)/shard_map/ppermute | solution.py:21
  170.9 9.7 %collective-permute-done.1 = f32[2,512,1,128]{1,3,2,0:T(8,128)S(1)} collective-permute-done((f32[2,512,1,128]{1,3,2,0:T(8,128)S(1)}, f32[2,512,1,128]{1,3,2,0:T(8,128)S(1)}, u32[]{:S(2)}, u32[]{:S(2)}) %collective-permute-start.1) | collective-permute-done | bytes 524320 | tf_op jit(solution)/shard_map/ppermute | solution.py:18
  180.6 2.9 %fusion.11 = f32[2,512,4,128]{1,3,2,0:T(8,128)S(1)} fusion(f32[2,512,1,128]{1,3,2,0:T(8,128)S(1)} %collective-permute-done.3, f32[1,512,4,128]{1,3,2,0:T(8,128)S(1)} %bitcast_add_fusion, f32[1,512,4,128]{1,3,2,0:T(8,128)S(1)} %bitcast_add_fusion.4, f32[2,512,1,128]{1,3,2,0:T(8,128)S(1)} %collective-permute-done.1, ...), kind=kLoop, calls=%fused_computation.30 | loop fusion | flops 15204352 | bytes 11545096 | tf_op jit(solution)/shard_map/add | solution.py:27
  184.4 1.8 copy.174
  (110 shorter events, 15.3 us)
Async XLA Ops:
  1.7 5.5 %copy-start.19 = (f32[4,128]{1,0:T(4,128)S(1)}, f32[4,128]{1,0:T(4,128)}, u32[]{:S(2)}) copy-start(f32[4,128]{1,0:T(4,128)} %param.14) | copy-start | bytes 6148
  1.7 11.1 %copy-start.20 = (s32[4]{0:T(128)S(1)}, s32[4]{0:T(128)}, u32[]{:S(2)}) copy-start(s32[4]{0:T(128)} %param.16) | copy-start | bytes 52
  3.1 61.2 %all-to-all-start = ((f32[512,2,256]{0,2,1:T(8,128)}), f32[512,2,256]{0,2,1:T(8,128)S(1)}, u32[]{:S(2)}, u32[]{:S(2)}) async-start(f32[512,2,256]{0,2,1:T(8,128)} %bitcast.6), calls=%async_computation | async-start | bytes 2097152 | tf_op jit(solution)/shard_map/all_to_all | solution.py:52
  7.2 81.7 %collective-permute-start = (f32[1,1,1,128]{3,2,1,0:T(1,128)S(1)}, f32[1,1,1,128]{3,2,1,0:T(1,128)S(1)}, u32[]{:S(2)}, u32[]{:S(2)}) collective-permute-start(f32[1,1,1,128]{3,2,1,0:T(1,128)S(1)} %get-tuple-element.56), channel_id=1, source_target_pairs={{0,1},{1,2},{2,3},{3,4},{4,5},{5,6},{6,7},{7,8},{8,9},{9,10},{10,1... | collective-permute-start | bytes 1544 | tf_op jit(solution)/shard_map/ppermute | solution.py:18
  9.1 79.7 %collective-permute-start.2 = (f32[1,1,1,128]{3,2,1,0:T(1,128)S(1)}, f32[1,1,1,128]{3,2,1,0:T(1,128)S(1)}, u32[]{:S(2)}, u32[]{:S(2)}) collective-permute-start(f32[1,1,1,128]{3,2,1,0:T(1,128)S(1)} %get-tuple-element.57), channel_id=1, source_target_pairs={{1,0},{2,1},{3,2},{4,3},{5,4},{6,5},{7,6},{8,7},{9,8},{10,9},{11,1... | collective-permute-start | bytes 1544 | tf_op jit(solution)/shard_map/ppermute | solution.py:21
  28.0 4.4 %copy-start.21 = (f32[4]{0:T(128)S(1)}, f32[4]{0:T(128)}, u32[]{:S(2)}) copy-start(f32[4]{0:T(128)} %param.17) | copy-start | bytes 52
  28.0 10.0 %copy-start.22 = (s32[4,128]{1,0:T(4,128)S(1)}, s32[4,128]{1,0:T(4,128)}, u32[]{:S(2)}) copy-start(s32[4,128]{1,0:T(4,128)} %param.15) | copy-start | bytes 6148
  32.1 8.9 %copy-start.23 = (s32[2,4]{1,0:T(2,128)S(1)}, s32[2,4]{1,0:T(2,128)}, u32[]{:S(2)}) copy-start(s32[2,4]{1,0:T(2,128)} %param.18) | copy-start | bytes 100
  41.1 6.3 %copy-start.7 = (bf16[1,1,512,4,128]{4,3,2,1,0:T(4,128)(2,1)S(1)}, bf16[1,1,512,4,128]{4,3,2,1,0:T(4,128)(2,1)}, u32[]{:S(2)}) copy-start(bf16[1,1,512,4,128]{4,3,2,1,0:T(4,128)(2,1)} %get-tuple-element.33) | copy-start | bytes 1572868
  45.2 5.4 %copy-start.6 = (bf16[1,1,512,4,128]{4,3,2,1,0:T(4,128)(2,1)S(1)}, bf16[1,1,512,4,128]{4,3,2,1,0:T(4,128)(2,1)}, u32[]{:S(2)}) copy-start(bf16[1,1,512,4,128]{4,3,2,1,0:T(4,128)(2,1)} %get-tuple-element.32) | copy-start | bytes 1572868
  50.6 7.6 %copy-start.5 = (bf16[1,1,512,4,128]{4,3,2,1,0:T(4,128)(2,1)S(1)}, bf16[1,1,512,4,128]{4,3,2,1,0:T(4,128)(2,1)}, u32[]{:S(2)}) copy-start(bf16[1,1,512,4,128]{4,3,2,1,0:T(4,128)(2,1)} %get-tuple-element.37) | copy-start | bytes 1572868
  53.9 7.7 %copy-start.4 = (bf16[1,1,512,4,128]{4,3,2,1,0:T(4,128)(2,1)S(1)}, bf16[1,1,512,4,128]{4,3,2,1,0:T(4,128)(2,1)}, u32[]{:S(2)}) copy-start(bf16[1,1,512,4,128]{4,3,2,1,0:T(4,128)(2,1)} %get-tuple-element.30) | copy-start | bytes 1572868
  59.4 3.4 %copy-start.8 = (bf16[1,1,512,4,128]{4,3,2,1,0:T(4,128)(2,1)S(1)}, bf16[1,1,512,4,128]{4,3,2,1,0:T(4,128)(2,1)}, u32[]{:S(2)}) copy-start(bf16[1,1,512,4,128]{4,3,2,1,0:T(4,128)(2,1)} %get-tuple-element.28) | copy-start | bytes 1572868
  66.9 22.0 %all-to-all-start.1 = ((f32[2,512,256]{2,1,0:T(8,128)}), f32[2,512,256]{2,1,0:T(8,128)S(1)}, u32[]{:S(2)}, u32[]{:S(2)}) async-start(f32[2,512,256]{2,1,0:T(8,128)} %bitcast.13), calls=%async_computation.1 | async-start | bytes 2097152 | tf_op jit(solution)/shard_map/all_to_all | solution.py:69
  80.2 4.4 %copy-start.3 = (bf16[1,1,512,4,128]{4,3,2,1,0:T(4,128)(2,1)S(1)}, bf16[1,1,512,4,128]{4,3,2,1,0:T(4,128)(2,1)}, u32[]{:S(2)}) copy-start(bf16[1,1,512,4,128]{4,3,2,1,0:T(4,128)(2,1)} %get-tuple-element.35) | copy-start | bytes 1572868
  80.2 7.6 %copy-start.2 = (bf16[1,1,512,4,128]{4,3,2,1,0:T(4,128)(2,1)S(1)}, bf16[1,1,512,4,128]{4,3,2,1,0:T(4,128)(2,1)}, u32[]{:S(2)}) copy-start(bf16[1,1,512,4,128]{4,3,2,1,0:T(4,128)(2,1)} %get-tuple-element.34) | copy-start | bytes 1572868
  99.7 5.3 %copy-start = (f32[1,512,4,128]{3,2,1,0:T(4,128)S(1)}, f32[1,512,4,128]{3,2,1,0:T(4,128)}, u32[]{:S(2)}) copy-start(f32[1,512,4,128]{3,2,1,0:T(4,128)} %copy.142) | copy-start | bytes 3145732
  99.7 5.3 %copy-start.1 = (f32[1,512,4,128]{3,2,1,0:T(4,128)S(1)}, f32[1,512,4,128]{3,2,1,0:T(4,128)}, u32[]{:S(2)}) copy-start(f32[1,512,4,128]{3,2,1,0:T(4,128)} %copy.144) | copy-start | bytes 3145732
  105.0 47.6 %copy-start.9 = (bf16[1,1,512,4,128]{2,4,3,1,0:T(8,128)(2,1)S(1)}, bf16[1,1,512,4,128]{2,4,3,1,0:T(8,128)(2,1)}, u32[]{:S(2)}) copy-start(bf16[1,1,512,4,128]{2,4,3,1,0:T(8,128)(2,1)} %copy.185) | copy-start | bytes 1572868
  105.0 47.6 %copy-start.11 = (bf16[1,1,512,4,128]{2,4,3,1,0:T(8,128)(2,1)S(1)}, bf16[1,1,512,4,128]{2,4,3,1,0:T(8,128)(2,1)}, u32[]{:S(2)}) copy-start(bf16[1,1,512,4,128]{2,4,3,1,0:T(8,128)(2,1)} %copy.186) | copy-start | bytes 1572868
  152.6 6.5 %copy-start.10 = (bf16[1,1,512,4,128]{2,4,3,1,0:T(8,128)(2,1)S(1)}, bf16[1,1,512,4,128]{2,4,3,1,0:T(8,128)(2,1)}, u32[]{:S(2)}) copy-start(bf16[1,1,512,4,128]{2,4,3,1,0:T(8,128)(2,1)} %copy.177) | copy-start | bytes 1572868
  152.6 6.5 %copy-start.12 = (bf16[1,1,512,4,128]{2,4,3,1,0:T(8,128)(2,1)S(1)}, bf16[1,1,512,4,128]{2,4,3,1,0:T(8,128)(2,1)}, u32[]{:S(2)}) copy-start(bf16[1,1,512,4,128]{2,4,3,1,0:T(8,128)(2,1)} %copy.178) | copy-start | bytes 1572868
  152.6 6.5 %copy-start.13 = (bf16[1,1,512,4,128]{2,4,3,1,0:T(8,128)(2,1)S(1)}, bf16[1,1,512,4,128]{2,4,3,1,0:T(8,128)(2,1)}, u32[]{:S(2)}) copy-start(bf16[1,1,512,4,128]{2,4,3,1,0:T(8,128)(2,1)} %copy.179) | copy-start | bytes 1572868
  152.6 6.5 %copy-start.14 = (bf16[1,1,512,4,128]{2,4,3,1,0:T(8,128)(2,1)S(1)}, bf16[1,1,512,4,128]{2,4,3,1,0:T(8,128)(2,1)}, u32[]{:S(2)}) copy-start(bf16[1,1,512,4,128]{2,4,3,1,0:T(8,128)(2,1)} %copy.180) | copy-start | bytes 1572868
  152.7 6.5 %copy-start.15 = (bf16[1,1,512,4,128]{2,4,3,1,0:T(8,128)(2,1)S(1)}, bf16[1,1,512,4,128]{2,4,3,1,0:T(8,128)(2,1)}, u32[]{:S(2)}) copy-start(bf16[1,1,512,4,128]{2,4,3,1,0:T(8,128)(2,1)} %copy.181) | copy-start | bytes 1572868
  152.7 6.5 %copy-start.16 = (bf16[1,1,512,4,128]{2,4,3,1,0:T(8,128)(2,1)S(1)}, bf16[1,1,512,4,128]{2,4,3,1,0:T(8,128)(2,1)}, u32[]{:S(2)}) copy-start(bf16[1,1,512,4,128]{2,4,3,1,0:T(8,128)(2,1)} %copy.182) | copy-start | bytes 1572868
  152.7 6.5 %copy-start.17 = (bf16[1,1,512,4,128]{2,4,3,1,0:T(8,128)(2,1)S(1)}, bf16[1,1,512,4,128]{2,4,3,1,0:T(8,128)(2,1)}, u32[]{:S(2)}) copy-start(bf16[1,1,512,4,128]{2,4,3,1,0:T(8,128)(2,1)} %copy.183) | copy-start | bytes 1572868
  152.7 6.5 %copy-start.18 = (bf16[1,1,512,4,128]{2,4,3,1,0:T(8,128)(2,1)S(1)}, bf16[1,1,512,4,128]{2,4,3,1,0:T(8,128)(2,1)}, u32[]{:S(2)}) copy-start(bf16[1,1,512,4,128]{2,4,3,1,0:T(8,128)(2,1)} %copy.184) | copy-start | bytes 1572868
  164.5 16.1 %collective-permute-start.1 = (f32[2,512,1,128]{1,3,2,0:T(8,128)S(1)}, f32[2,512,1,128]{1,3,2,0:T(8,128)S(1)}, u32[]{:S(2)}, u32[]{:S(2)}) collective-permute-start(f32[2,512,1,128]{1,3,2,0:T(8,128)S(1)} %get-tuple-element.44), channel_id=1, source_target_pairs={{0,1},{1,2},{2,3},{3,4},{4,5},{5,6},{6,7},{7,8},{8,9},{9,10},{10,1... | collective-permute-start | bytes 1572872 | tf_op jit(solution)/shard_map/ppermute | solution.py:18
  166.4 14.2 %collective-permute-start.3 = (f32[2,512,1,128]{1,3,2,0:T(8,128)S(1)}, f32[2,512,1,128]{1,3,2,0:T(8,128)S(1)}, u32[]{:S(2)}, u32[]{:S(2)}) collective-permute-start(f32[2,512,1,128]{1,3,2,0:T(8,128)S(1)} %get-tuple-element.45), channel_id=1, source_target_pairs={{1,0},{2,1},{3,2},{4,3},{5,4},{6,5},{7,6},{8,7},{9,8},{10,9},{11,1... | collective-permute-start | bytes 1572872 | tf_op jit(solution)/shard_map/ppermute | solution.py:21
